TPU v7x, 256 devices: a whole 4x4x8 slice. The times are simulated.
256 devices in a mesh: dp: 32 (over x_hi, z, core), mp: 8 (over x_lo, y).
Axes of the slice: x: 4 (x_hi: 2, x_lo: 2; x = x_hi * 2 + x_lo), y: 4, z: 8, core: 2. Of those that a mesh axis runs over, the one named last changes fastest.
Arguments:
- context: bfloat16 [8192, 6144], P('dp', 'mp'), may hold values from -6 to 6
- out_grad: bfloat16 [8192, 6144], P('dp', 'mp'), may hold values from -1.0546875 to 1.0546875
- master: float32 [8, 36864, 128], P('mp', 'dp'), may hold values from -0.078125 to 0.078125
- moment_one: float32 [8, 36864, 128], P('mp', 'dp'), may hold values from -3 to 3
- moment_two: float32 [8, 36864, 128], P('mp', 'dp'), may hold values from 1 to 64
- new_owner: int32 [32], replicated, may hold values from 0 to 31, as said below
- old_pieces: int32 [32, 32, 36], replicated, may hold values from 0 to 36863, as said below
Outputs:
- proj_out: bfloat16 [8192, 6144], P('dp', 'mp')
- master_out: float32 [8, 36864, 128], P('mp', 'dp')
- moment_one_out: float32 [8, 36864, 128], P('mp', 'dp')
- moment_two_out: float32 [8, 36864, 128], P('mp', 'dp')
Inputs may be any that keep to these rules, and one draw needn't show every extreme that they name: `new_owner`: each index of dp appears exactly once. Every block number appears exactly once; old_pieces[i, j, :] lie from new_owner[j] * 1152 to new_owner[j] * 1152 + 1151.
All inputs are finite; a program needn't handle non-finite values.
Results may differ from a plain program's by a relative error of at most 0.015.
Values may be sent and summed in bfloat16 or wider, within the bound.
No kernel may reach another device: no remote copies, remote signals or barrier semaphores. Data moves between devices by JAX's collectives and lax.ppermute only.
A program may use at most 64 MiB of HBM per device.

v0:
```python
import jax
import jax.numpy as jnp
from jax import lax
from jax.sharding import Mesh, PartitionSpec as P

beta_one = 0.9
beta_two = 0.999
learn_rate = 0.001
decay_rate = 0.1
epsilon = 1e-08
step_count = 100.0
DP = ("xh", "z", "c")
MP = ("xl", "y")
DL = ("xh", "c")


def adamw(weights, first_moment, second_moment, gradient):
    first_new = beta_one * first_moment + (1.0 - beta_one) * gradient
    second_new = beta_two * second_moment + (1.0 - beta_two) * gradient * gradient
    corrected_first = first_new / (1.0 - beta_one**step_count)
    corrected_second = second_new / (1.0 - beta_two**step_count)
    update = corrected_first / (jnp.sqrt(corrected_second) + epsilon)
    weights_new = weights - learn_rate * (update + decay_rate * weights)
    return (weights_new, first_new, second_new)


def one_hot(index, count):
    rows = lax.broadcasted_iota(jnp.int32, (count, index.shape[0]), 0)
    return (rows == index[None, :]).astype(jnp.bfloat16)


def local(context, out_grad, master, moment_one, moment_two, new_owner, old_pieces):
    f32, bf16 = (jnp.float32, jnp.bfloat16)
    n_dp, n_mp = (lax.axis_size(DP), lax.axis_size(MP))
    n_z, n_dl = (lax.axis_size("z"), lax.axis_size(DL))
    n_xh, n_c = (lax.axis_size("xh"), lax.axis_size("c"))
    d = lax.axis_index(DP)
    blocks, width = master.shape[1:]
    tokens, cols = context.shape
    per_dev = cols // width
    per_row = per_dev * n_mp
    rows = blocks // per_row
    own_slab = new_owner[d]
    positions = (
        lax.dynamic_index_in_dim(old_pieces, d, 1, keepdims=False) - own_slab * blocks
    ).reshape(-1)
    w_in = lax.all_to_all(master[0].astype(bf16), DP, 0, 0, tiled=True)
    moments = jnp.concatenate([moment_one[0], moment_two[0]], axis=1).astype(bf16)
    m_in = lax.all_to_all(moments, DP, 0, 0, tiled=True)
    owner_order = new_owner.reshape(n_xh, n_z, n_c).transpose(0, 2, 1).reshape(-1)
    wanted = (owner_order[:, None] * rows + jnp.arange(rows, dtype=jnp.int32)[None]).reshape(-1)
    columns = lax.broadcasted_iota(jnp.int32, (cols, cols), 1)
    select = (columns == wanted[:, None]).astype(bf16)
    ct = lax.dot_general(
        select, context, (((1,), (1,)), ((), ())), preferred_element_type=f32
    ).astype(bf16)
    ct = lax.all_to_all(ct.reshape(n_dl, n_z * rows, tokens), DL, 0, 0, tiled=True)
    ct = lax.all_gather(ct, MP, axis=0, tiled=False)
    ct = (
        ct.reshape(n_mp, n_dl, n_z, rows, tokens)
        .transpose(0, 2, 3, 1, 4)
        .reshape(n_mp * n_z * rows, n_dl * tokens)
    )
    og = lax.all_gather(out_grad, DL, axis=0, tiled=True)
    grad = jnp.dot(ct, og, preferred_element_type=f32).astype(bf16)
    grad = lax.psum_scatter(
        grad.reshape(n_mp, n_z, rows, cols), "z", scatter_dimension=1, tiled=True
    )
    grad = lax.all_to_all(grad.reshape(n_mp, rows, cols), MP, 0, 0, tiled=True)
    grad = (
        grad.reshape(n_mp, rows, per_dev, width)
        .transpose(1, 0, 2, 3)
        .reshape(blocks, width)
        .astype(f32)
    )
    w_at = positions % per_row * rows + positions // per_row
    w_t = jnp.dot(one_hot(w_at, blocks), w_in, preferred_element_type=f32).astype(bf16)
    w_t = lax.all_to_all(w_t.reshape(n_mp, per_dev, rows, width), MP, 0, 0, tiled=True)
    w_t = lax.all_gather(w_t, "z", axis=0, tiled=False)
    w_t = w_t.transpose(1, 0, 3, 2, 4).reshape(n_mp * n_z * rows, cols)
    out = lax.dot_general(ct, w_t, (((0,), (0,)), ((), ())), preferred_element_type=f32).astype(
        bf16
    )
    proj_out = lax.psum_scatter(out, DL, scatter_dimension=0, tiled=True)
    placed = jnp.dot(
        one_hot(positions, blocks),
        jnp.concatenate([w_in, m_in], axis=1),
        preferred_element_type=f32,
    )
    weights, first_moment, second_moment = (
        placed[:, i * width : (i + 1) * width] for i in range(3)
    )
    weights_new, first_new, second_new = adamw(weights, first_moment, second_moment, grad)
    return (proj_out, weights_new[None], first_new[None], second_new[None])


def solution(mesh):
    fine = Mesh(mesh.devices.reshape(2, 8, 2, 2, 4), DP[:2] + ("c",) + MP)
    placed = (P(DP, MP), P(DP, MP), P(MP, DP, None), P(MP, DP, None), P(MP, DP, None), P(), P())
    return jax.shard_map(
        local,
        mesh=fine,
        in_specs=placed,
        out_specs=(P(DP, MP), P(MP, DP, None), P(MP, DP, None), P(MP, DP, None)),
        check_vma=False,
    )
```

profile of v0, /device:TPU:1, one launch (start us, length us, event | category | flops | bytes accessed | tf_op | source)
XLA Modules:
  0.0 251.5 jit_solution(14708763887175539069)
XLA Ops:
  7.2 0.7 broadcast_multiply_fusion
  8.3 0.1 add.75
  8.4 0.6 fusion.12
  9.0 14.1 %all_to_all.33 = bf16[4,192,256]{2,1,0:T(8,128)(2,1)} all-to-all(bf16[4,192,256]{2,1,0:T(8,128)(2,1)S(1)} %bitcast.42), channel_id=1, replica_groups=mesh['xh'=2,'z'=8,'c'=2,'xl'=2,'y'=4] {'xh','c'}, dimensions={0} | all-to-all | bytes 786432 | tf_op jit(solution)/shard_map/all_to_all | solution.py:57
  23.2 0.7 all-gather.6.cloned.1.call-update
  24.0 0.8 convert_element_type.38
  24.8 9.1 %all-to-all-start.1 = ((bf16[32,36,128]{2,1,0:T(8,128)(2,1)}), bf16[32,36,128]{2,1,0:T(8,128)(2,1)S(1)}, u32[]{:S(2)}, u32[]{:S(2)}) async-start(bf16[32,36,128]{2,1,0:T(8,128)(2,1)} %convert_element_type.38), calls=%async_computation.1 | async-start | bytes 655360 | tf_op jit(solution)/shard_map/all_to_all | solution.py:47
  33.9 0.6 dynamic_slice.8
  35.2 1.0 subtract_reduce_fusion
  36.1 0.1 sub.28
  36.3 12.1 %all-to-all-done.1 = bf16[32,36,128]{2,1,0:T(8,128)(2,1)S(1)} async-done(((bf16[32,36,128]{2,1,0:T(8,128)(2,1)}), bf16[32,36,128]{2,1,0:T(8,128)(2,1)S(1)}, u32[]{:S(2)}, u32[]{:S(2)}) %all-to-all-start.1) | async-done | bytes 294944 | tf_op jit(solution)/shard_map/all_to_all | solution.py:47
  48.4 1.0 fusion.4
  49.5 16.6 %all_to_all.34 = bf16[8,6,24,128]{3,2,1,0:T(8,128)(2,1)} all-to-all(bf16[8,6,24,128]{3,2,1,0:T(8,128)(2,1)S(1)} %bitcast.44), channel_id=1, replica_groups=mesh['xh'=2,'z'=8,'c'=2,'xl'=2,'y'=4] {'xl','y'}, dimensions={0} | all-to-all | bytes 589824 | tf_op jit(solution)/shard_map/all_to_all | solution.py:78
  66.1 8.6 %all-gather.8.cloned.1.call-done = bf16[32,192,256]{2,1,0:T(8,128)(2,1)} async-done(((bf16[4,192,256]{2,1,0:T(8,128)(2,1)}), bf16[32,192,256]{2,1,0:T(8,128)(2,1)}) %all-gather.8.cloned.1.call-update) | async-done | bytes 3145744 | tf_op jit(solution)/shard_map/all_gather | solution.py:58
  74.7 5.9 %copy.22 = bf16[8,8,24,4,256]{4,3,2,1,0:T(4,128)(2,1)S(1)} copy(bf16[8,8,24,4,256]{4,2,1,3,0:T(8,128)(2,1)} %bitcast.35) | data formatting | bytes 6291456 | tf_op jit(solution)/shard_map/transpose | solution.py:61
  80.6 0.8 copy.26
  81.4 22.4 %all-gather.6.cloned.1.call-done = bf16[1024,768]{1,0:T(8,128)(2,1)} async-done(((bf16[256,768]{1,0:T(8,128)(2,1)}), bf16[1024,768]{1,0:T(8,128)(2,1)}) %all-gather.6.cloned.1.call-update) | async-done | bytes 1572880 | tf_op jit(solution)/shard_map/all_gather | solution.py:64
  103.7 4.2 %convolution_convert_fusion = bf16[1536,768]{1,0:T(8,128)(2,1)S(1)} fusion(bf16[1536,1024]{1,0:T(8,128)(2,1)S(1)} %bitcast.36, bf16[1024,768]{1,0:T(8,128)(2,1)} %all-gather.6.cloned.1.call-done), kind=kOutput, calls=%fused_computation.4 | convolution fusion | flops 2417098752 | bytes 7077888 | tf_op jit(solution)/shard_map/dot_general | solution.py:65
  107.9 1.6 copy.24
  109.6 32.6 %all-gather.10.cloned.1.call-done = bf16[64,6,24,128]{3,2,1,0:T(8,128)(2,1)} async-done(((bf16[8,6,24,128]{3,2,1,0:T(8,128)(2,1)}), bf16[64,6,24,128]{3,2,1,0:T(8,128)(2,1)}) %all-gather.10.cloned.1.call-update) | async-done | bytes 2359312 | tf_op jit(solution)/shard_map/all_gather | solution.py:79
  142.2 2.5 %copy.23 = bf16[8,8,24,6,128]{4,3,2,1,0:T(8,128)(2,1)S(1)} copy(bf16[8,8,24,6,128]{4,2,3,0,1:T(8,128)(2,1)} %bitcast.41) | data formatting | bytes 4718592 | tf_op jit(solution)/shard_map/transpose | solution.py:80
  144.7 3.9 %fusion.9 = bf16[1024,768]{1,0:T(8,128)(2,1)} fusion(bf16[1536,1024]{1,0:T(8,128)(2,1)S(1)} %bitcast.37, bf16[192,8,6,128]{3,2,1,0:T(8,128)(2,1)S(1)} %bitcast.39), kind=kOutput, calls=%fused_computation.13 | convolution fusion | flops 2416705536 | bytes 7077888 | tf_op jit(solution)/shard_map/dot_general | solution.py:81
  148.6 1.2 convert.12
  150.1 39.4 %all_to_all.35 = bf16[32,36,256]{2,1,0:T(8,128)(2,1)S(1)} all-to-all(bf16[32,36,256]{2,1,0:T(8,128)(2,1)S(1)} %pad_maximum_fusion), channel_id=1, replica_groups=mesh['xh'=2,'z'=8,'c'=2,'xl'=2,'y'=4] {'xh','z','c'}, dimensions={0} | all-to-all | bytes 1179648 | tf_op jit(solution)/shard_map/all_to_all | solution.py:49
  189.4 0.1 all_to_all.26
  189.6 9.6 %reduce-scatter.5.cloned.1.call-done = bf16[8,1,24,768]{3,2,0,1:T(8,128)(2,1)} async-done(((bf16[8,8,24,768]{3,2,0,1:T(8,128)(2,1)}), bf16[8,1,24,768]{3,2,0,1:T(8,128)(2,1)}) %reduce-scatter.5.cloned.1.call-update) | async-done | bytes 294928 | tf_op jit(solution)/shard_map/reduce_scatter | solution.py:66
  199.2 4.8 %all-to-all-start.4 = ((bf16[8,24,768]{2,1,0:T(8,128)(2,1)}), bf16[8,24,768]{2,1,0:T(8,128)(2,1)S(1)}, u32[]{:S(2)}, u32[]{:S(2)}) async-start(bf16[8,24,768]{2,1,0:T(8,128)(2,1)} %bitcast.43), calls=%async_computation.6 | async-start | bytes 589824 | tf_op jit(solution)/shard_map/all_to_all | solution.py:69
  204.0 2.8 %fusion.1 = f32[1152,384]{1,0:T(8,128)} fusion(s32[1152]{0:T(1024)S(1)} %sub.28, bf16[1152,256]{1,0:T(8,128)(2,1)S(1)} %all_to_all.26, bf16[1152,128]{1,0:T(8,128)(2,1)S(1)} %copy-done.4), kind=kOutput, calls=%fused_computation.3 | convolution fusion | flops 1022312448 | bytes 2658816 | tf_op jit(solution)/shard_map/dot_general | solution.py:85
  206.8 3.4 %all-to-all-done.4 = bf16[8,24,768]{2,1,0:T(8,128)(2,1)S(1)} async-done(((bf16[8,24,768]{2,1,0:T(8,128)(2,1)}), bf16[8,24,768]{2,1,0:T(8,128)(2,1)S(1)}, u32[]{:S(2)}, u32[]{:S(2)}) %all-to-all-start.4) | async-done | bytes 294944 | tf_op jit(solution)/shard_map/all_to_all | solution.py:69
  210.2 0.3 reshape.109
  210.7 2.9 %fusion.20 = (f32[1,1152,128]{2,1,0:T(8,128)}, f32[1,1152,128]{2,1,0:T(8,128)}, f32[1,1152,128]{2,1,0:T(8,128)}) fusion(f32[1152,128]{1,0:T(8,128)S(1)} %reshape.108, f32[1152,384]{1,0:T(8,128)} %fusion.1), kind=kLoop, calls=%fused_computation.27 | loop fusion | flops 2211840 | bytes 4128768 | tf_op jit(solution)/shard_map/broadcast_in_dim | solution.py:94
  213.6 31.3 %reduce-scatter.3.cloned.1.call-done = bf16[256,768]{1,0:T(8,128)(2,1)} async-done(((bf16[1024,768]{1,0:T(8,128)(2,1)}), bf16[256,768]{1,0:T(8,128)(2,1)}) %reduce-scatter.3.cloned.1.call-update) | async-done | bytes 393232 | tf_op jit(solution)/shard_map/reduce_scatter | solution.py:84
  (34 shorter events, 1.1 us)
Async XLA Ops:
  7.2 1.2 copy-start
  7.2 16.8 %copy-start.1 = (f32[1,1152,128]{2,1,0:T(8,128)S(1)}, f32[1,1152,128]{2,1,0:T(8,128)}, u32[]{:S(2)}) copy-start(f32[1,1152,128]{2,1,0:T(8,128)} %param.9) | copy-start | bytes 1769476
  7.2 67.5 %all-gather.8.cloned.1.call-start = ((), (), s32[]{:S(2)}) async-start(), calls=%async_computation.10 | async-start | bytes 3538944 | tf_op jit(solution)/shard_map/all_gather | solution.py:58
  8.4 25.5 %copy-start.5 = (s32[32]{0:T(128)S(1)}, s32[32]{0:T(128)}, u32[]{:S(2)}) copy-start(s32[32]{0:T(128)} %param.12) | copy-start | bytes 388
  23.2 80.6 %all-gather.6.cloned.1.call-start = ((), (), s32[]{:S(2)}) async-start(), calls=%async_computation.8 | async-start | bytes 1966080 | tf_op jit(solution)/shard_map/all_gather | solution.py:64
  24.8 23.6 %all-to-all-start.1 = ((bf16[32,36,128]{2,1,0:T(8,128)(2,1)}), bf16[32,36,128]{2,1,0:T(8,128)(2,1)S(1)}, u32[]{:S(2)}, u32[]{:S(2)}) async-start(bf16[32,36,128]{2,1,0:T(8,128)(2,1)} %convert_element_type.38), calls=%async_computation.1 | async-start | bytes 655360 | tf_op jit(solution)/shard_map/all_to_all | solution.py:47
  33.8 108.4 %all-gather.10.cloned.1.call-start = ((), (), s32[]{:S(2)}) async-start(), calls=%async_computation.11 | async-start | bytes 2654208 | tf_op jit(solution)/shard_map/all_gather | solution.py:79
  48.4 32.2 %copy-start.3 = (bf16[1152,128]{1,0:T(8,128)(2,1)}, bf16[1152,128]{1,0:T(8,128)(2,1)S(1)}, u32[]{:S(2)}) copy-start(bf16[1152,128]{1,0:T(8,128)(2,1)S(1)} %all_to_all.23) | copy-start | bytes 884740
  66.0 133.2 %reduce-scatter.5.cloned.1.call-start = ((), (), s32[]{:S(2)}) async-start(), calls=%async_computation.9 | async-start | bytes 2654208 | tf_op jit(solution)/shard_map/reduce_scatter | solution.py:66
  109.6 135.3 %reduce-scatter.3.cloned.1.call-start = ((), (), s32[]{:S(2)}) async-start(), calls=%async_computation.7 | async-start | bytes 1966080 | tf_op jit(solution)/shard_map/reduce_scatter | solution.py:84
  148.6 1.2 copy-start.2
  150.0 54.0 %copy-start.4 = (bf16[1152,128]{1,0:T(8,128)(2,1)S(1)}, bf16[1152,128]{1,0:T(8,128)(2,1)}, u32[]{:S(2)}) copy-start(bf16[1152,128]{1,0:T(8,128)(2,1)} %copy-done.3) | copy-start | bytes 884740
  199.2 11.0 %all-to-all-start.4 = ((bf16[8,24,768]{2,1,0:T(8,128)(2,1)}), bf16[8,24,768]{2,1,0:T(8,128)(2,1)S(1)}, u32[]{:S(2)}, u32[]{:S(2)}) async-start(bf16[8,24,768]{2,1,0:T(8,128)(2,1)} %bitcast.43), calls=%async_computation.6 | async-start | bytes 589824 | tf_op jit(solution)/shard_map/all_to_all | solution.py:69
Sparse Core Ops, SparseCore 0:
  23.3 51.3 all-gather.7
  76.5 27.2 all-gather.5
  105.5 36.6 all-gather.9
  144.6 54.5 reduce-scatter.4
  202.4 42.4 reduce-scatter.2
where the time goes:
time: 252 us; the launch traced here: 251 us
  waiting for transfers between devices  121 us (48%)
  blocking collectives  70.1 us (28%)
  between operations  14.7 us (6%)
  starting transfers between devices  14 us (6%)
  local copies, waits for them, and re-layouts  13.5 us (5%)
  matrix products  12.5 us (5%)
  other arithmetic  6.02 us (2%)
    all_to_all x1, blocking collectives, local(): m_in = lax.all_to_all(moments, DP, 0, 0, tiled=True)  39.4 us
    all_gather x1, waiting for transfers between devices, local(): w_t = lax.all_gather(w_t, 'z', axis=0, tiled=False)  32.6 us
    reduce_scatter x1, waiting for transfers between devices, local(): proj_out = lax.psum_scatter(out, DL, scatter_dimension=0, tiled=True)  31.3 us
    all_gather x1, waiting for transfers between devices, local(): og = lax.all_gather(out_grad, DL, axis=0, tiled=True)  22.4 us
    all_to_all x1, blocking collectives, local(): lax.all_to_all(w_t.reshape(n_mp, per_dev, rows, width), MP, 0, 0, tiled=T...  16.6 us
    all_to_all x1, blocking collectives, local(): lax.all_to_all(ct.reshape(n_dl, n_z * rows, tokens), DL, 0, 0, tiled=True)  14.1 us
    all_to_all x1, waiting for transfers between devices, local(): w_in = lax.all_to_all(master[0].astype(bf16), DP, 0, 0, tiled=True)  12.1 us
    reduce_scatter x1, waiting for transfers between devices, local(): lax.psum_scatter(grad.reshape(n_mp, n_z, rows, cols), 'z', scatter_dimens...  9.64 us
  transfers between devices with their start and end apart: 7, of which 7 were waited for; matrix products, arithmetic and copies ran while one was open for 12% of the time, Pallas kernels for 0%

commit v1 on v0

--- a/solution.py
+++ b/solution.py
@@ -61,7 +61,9 @@
         .transpose(0, 2, 3, 1, 4)
         .reshape(n_mp * n_z * rows, n_dl * tokens)
     )
-    og = lax.all_gather(out_grad, DL, axis=0, tiled=True)
+    og = jnp.concatenate(
+        lax.all_to_all(jnp.stack([out_grad] * lax.axis_size(DL)), DL, 0, 0), axis=0
+    )
     grad = jnp.dot(ct, og, preferred_element_type=f32).astype(bf16)
     grad = lax.psum_scatter(
         grad.reshape(n_mp, n_z, rows, cols), "z", scatter_dimension=1, tiled=True

time: 252 us -> 229 us (0.909)
  waiting for transfers between devices: 121 us -> 90.7 us
  starting transfers between devices: 14 us -> 19.3 us
    all_gather x1 -> x0, waiting for transfers between devices: 22.4 us -> none  [local(): og = lax.all_gather(out_grad, DL, axis=0, tiled=True)]
    all_gather x1, waiting for transfers between devices: 32.6 us -> 19.8 us  [local(): w_t = lax.all_gather(w_t, 'z', axis=0, tiled=False)]
    all_to_all x0 -> x1, waiting for transfers between devices: none -> 11.9 us  [local(): lax.all_to_all(jnp.stack([out_grad] * lax.axis_size(DL)), DL, 0, 0)]
    all_gather x1, waiting for transfers between devices: 8.58 us -> 2.7 us  [local(): ct = lax.all_gather(ct, MP, axis=0, tiled=False)]
    all_to_all x0 -> x1, starting transfers between devices: none -> 5.12 us  [local(): lax.all_to_all(jnp.stack([out_grad] * lax.axis_size(DL)), DL, 0, 0)]
  transfers between devices with their start and end apart: 7 -> 7, of which waited for: 7 -> 7; matrix products, arithmetic and copies ran while one was open for 12% -> 14% of each run, Pallas kernels for 0% -> 0%
where the time goes in v1:
time: 229 us; the launch traced here: 228 us
  waiting for transfers between devices  90.7 us (40%)
  blocking collectives  70.1 us (31%)
  starting transfers between devices  19.3 us (8%)
  local copies, waits for them, and re-layouts  14.8 us (6%)
  between operations  14.6 us (6%)
  matrix products  12.5 us (5%)
  other arithmetic  6.04 us (3%)
    all_to_all x1, blocking collectives, local(): m_in = lax.all_to_all(moments, DP, 0, 0, tiled=True)  39.4 us
    reduce_scatter x1, waiting for transfers between devices, local(): proj_out = lax.psum_scatter(out, DL, scatter_dimension=0, tiled=True)  31.1 us
    all_gather x1, waiting for transfers between devices, local(): w_t = lax.all_gather(w_t, 'z', axis=0, tiled=False)  19.8 us
    all_to_all x1, blocking collectives, local(): lax.all_to_all(w_t.reshape(n_mp, per_dev, rows, width), MP, 0, 0, tiled=T...  16.5 us
    all_to_all x1, blocking collectives, local(): lax.all_to_all(ct.reshape(n_dl, n_z * rows, tokens), DL, 0, 0, tiled=True)  14.2 us
    all_to_all x1, waiting for transfers between devices, local(): w_in = lax.all_to_all(master[0].astype(bf16), DP, 0, 0, tiled=True)  12.1 us
    all_to_all x1, waiting for transfers between devices, local(): lax.all_to_all(jnp.stack([out_grad] * lax.axis_size(DL)), DL, 0, 0)  11.9 us
    reduce_scatter x1, waiting for transfers between devices, local(): lax.psum_scatter(grad.reshape(n_mp, n_z, rows, cols), 'z', scatter_dimens...  9.7 us
  transfers between devices with their start and end apart: 7, of which 7 were waited for; matrix products, arithmetic and copies ran while one was open for 14% of the time, Pallas kernels for 0%

profile of v1, /device:TPU:1, one launch (start us, length us, event | category | flops | bytes accessed | tf_op | source)
XLA Modules:
  0.0 228.1 jit_solution(5758278040559627454)
XLA Ops:
  7.2 0.7 broadcast_multiply_fusion
  8.4 0.6 fusion.12
  9.0 14.2 %all_to_all.38 = bf16[4,192,256]{2,1,0:T(8,128)(2,1)} all-to-all(bf16[4,192,256]{2,1,0:T(8,128)(2,1)S(1)} %bitcast.43), channel_id=1, replica_groups=mesh['xh'=2,'z'=8,'c'=2,'xl'=2,'y'=4] {'xh','c'}, dimensions={0} | all-to-all | bytes 786432 | tf_op jit(solution)/shard_map/all_to_all | solution.py:57
  23.2 0.8 convert_element_type.38
  24.0 9.2 %all-to-all-start.1 = ((bf16[32,36,128]{2,1,0:T(8,128)(2,1)}), bf16[32,36,128]{2,1,0:T(8,128)(2,1)S(1)}, u32[]{:S(2)}, u32[]{:S(2)}) async-start(bf16[32,36,128]{2,1,0:T(8,128)(2,1)} %convert_element_type.38), calls=%async_computation.1 | async-start | bytes 655360 | tf_op jit(solution)/shard_map/all_to_all | solution.py:47
  33.3 0.6 dynamic_slice.8
  34.5 1.0 subtract_reduce_fusion
  35.6 12.1 %all-to-all-done.1 = bf16[32,36,128]{2,1,0:T(8,128)(2,1)S(1)} async-done(((bf16[32,36,128]{2,1,0:T(8,128)(2,1)}), bf16[32,36,128]{2,1,0:T(8,128)(2,1)S(1)}, u32[]{:S(2)}, u32[]{:S(2)}) %all-to-all-start.1) | async-done | bytes 294944 | tf_op jit(solution)/shard_map/all_to_all | solution.py:47
  47.8 1.0 fusion.4
  48.8 16.5 %all_to_all.39 = bf16[8,6,24,128]{3,2,1,0:T(8,128)(2,1)} all-to-all(bf16[8,6,24,128]{3,2,1,0:T(8,128)(2,1)S(1)} %bitcast.45), channel_id=1, replica_groups=mesh['xh'=2,'z'=8,'c'=2,'xl'=2,'y'=4] {'xl','y'}, dimensions={0} | all-to-all | bytes 589824 | tf_op jit(solution)/shard_map/all_to_all | solution.py:80
  65.4 1.3 stack.2
  66.7 5.1 %all-to-all-start.4 = ((bf16[4,256,768]{2,1,0:T(8,128)(2,1)}), bf16[4,256,768]{2,1,0:T(8,128)(2,1)}, u32[]{:S(2)}, u32[]{:S(2)}) async-start(bf16[4,256,768]{2,1,0:T(8,128)(2,1)} %stack.2), calls=%async_computation.5 | async-start | bytes 3145728 | tf_op jit(solution)/shard_map/all_to_all | solution.py:65
  71.8 2.7 %all-gather.5.cloned.1.call-done = bf16[32,192,256]{2,1,0:T(8,128)(2,1)} async-done(((bf16[4,192,256]{2,1,0:T(8,128)(2,1)}), bf16[32,192,256]{2,1,0:T(8,128)(2,1)}) %all-gather.5.cloned.1.call-update) | async-done | bytes 3145744 | tf_op jit(solution)/shard_map/all_gather | solution.py:58
  74.5 5.9 %copy.22 = bf16[8,8,24,4,256]{4,3,2,1,0:T(4,128)(2,1)S(1)} copy(bf16[8,8,24,4,256]{4,2,1,3,0:T(8,128)(2,1)} %bitcast.36) | data formatting | bytes 6291456 | tf_op jit(solution)/shard_map/transpose | solution.py:61
  80.5 0.8 copy.26
  81.3 11.9 %all-to-all-done.4 = bf16[4,256,768]{2,1,0:T(8,128)(2,1)} async-done(((bf16[4,256,768]{2,1,0:T(8,128)(2,1)}), bf16[4,256,768]{2,1,0:T(8,128)(2,1)}, u32[]{:S(2)}, u32[]{:S(2)}) %all-to-all-start.4) | async-done | bytes 1572896 | tf_op jit(solution)/shard_map/all_to_all | solution.py:65
  93.2 4.2 %convolution_convert_fusion = bf16[1536,768]{1,0:T(8,128)(2,1)S(1)} fusion(bf16[1536,1024]{1,0:T(8,128)(2,1)S(1)} %bitcast.37, bf16[1024,768]{1,0:T(8,128)(2,1)} %bitcast.8), kind=kOutput, calls=%fused_computation.4 | convolution fusion | flops 2417098752 | bytes 7077888 | tf_op jit(solution)/shard_map/dot_general | solution.py:67
  97.4 1.6 copy.24
  99.0 0.2 reduce-scatter.3.cloned.1.call-start
  99.2 19.8 %all-gather.7.cloned.1.call-done = bf16[64,6,24,128]{3,2,1,0:T(8,128)(2,1)} async-done(((bf16[8,6,24,128]{3,2,1,0:T(8,128)(2,1)}), bf16[64,6,24,128]{3,2,1,0:T(8,128)(2,1)}) %all-gather.7.cloned.1.call-update) | async-done | bytes 2359312 | tf_op jit(solution)/shard_map/all_gather | solution.py:81
  119.0 2.5 %copy.23 = bf16[8,8,24,6,128]{4,3,2,1,0:T(8,128)(2,1)S(1)} copy(bf16[8,8,24,6,128]{4,2,3,0,1:T(8,128)(2,1)} %bitcast.42) | data formatting | bytes 4718592 | tf_op jit(solution)/shard_map/transpose | solution.py:82
  121.6 3.9 %fusion.9 = bf16[1024,768]{1,0:T(8,128)(2,1)} fusion(bf16[1536,1024]{1,0:T(8,128)(2,1)S(1)} %bitcast.38, bf16[192,8,6,128]{3,2,1,0:T(8,128)(2,1)S(1)} %bitcast.40), kind=kOutput, calls=%fused_computation.13 | convolution fusion | flops 2416705536 | bytes 7077888 | tf_op jit(solution)/shard_map/dot_general | solution.py:83
  125.5 1.2 convert.12
  126.9 39.4 %all_to_all.40 = bf16[32,36,256]{2,1,0:T(8,128)(2,1)S(1)} all-to-all(bf16[32,36,256]{2,1,0:T(8,128)(2,1)S(1)} %pad_maximum_fusion), channel_id=1, replica_groups=mesh['xh'=2,'z'=8,'c'=2,'xl'=2,'y'=4] {'xh','z','c'}, dimensions={0} | all-to-all | bytes 1179648 | tf_op jit(solution)/shard_map/all_to_all | solution.py:49
  166.3 0.1 all_to_all.29
  166.4 9.7 %reduce-scatter.5.cloned.1.call-done = bf16[8,1,24,768]{3,2,0,1:T(8,128)(2,1)} async-done(((bf16[8,8,24,768]{3,2,0,1:T(8,128)(2,1)}), bf16[8,1,24,768]{3,2,0,1:T(8,128)(2,1)}) %reduce-scatter.5.cloned.1.call-update) | async-done | bytes 294928 | tf_op jit(solution)/shard_map/reduce_scatter | solution.py:68
  176.1 4.7 %all-to-all-start.5 = ((bf16[8,24,768]{2,1,0:T(8,128)(2,1)}), bf16[8,24,768]{2,1,0:T(8,128)(2,1)S(1)}, u32[]{:S(2)}, u32[]{:S(2)}) async-start(bf16[8,24,768]{2,1,0:T(8,128)(2,1)} %bitcast.44), calls=%async_computation.7 | async-start | bytes 589824 | tf_op jit(solution)/shard_map/all_to_all | solution.py:71
  180.8 2.8 %fusion.1 = f32[1152,384]{1,0:T(8,128)} fusion(s32[1152]{0:T(1024)S(1)} %sub.28, bf16[1152,256]{1,0:T(8,128)(2,1)S(1)} %all_to_all.29, bf16[1152,128]{1,0:T(8,128)(2,1)S(1)} %copy-done.5), kind=kOutput, calls=%fused_computation.3 | convolution fusion | flops 1022312448 | bytes 2658816 | tf_op jit(solution)/shard_map/dot_general | solution.py:87
  183.6 3.4 %all-to-all-done.5 = bf16[8,24,768]{2,1,0:T(8,128)(2,1)S(1)} async-done(((bf16[8,24,768]{2,1,0:T(8,128)(2,1)}), bf16[8,24,768]{2,1,0:T(8,128)(2,1)S(1)}, u32[]{:S(2)}, u32[]{:S(2)}) %all-to-all-start.5) | async-done | bytes 294944 | tf_op jit(solution)/shard_map/all_to_all | solution.py:71
  187.0 0.3 reshape.115
  187.5 2.9 %fusion.20 = (f32[1,1152,128]{2,1,0:T(8,128)}, f32[1,1152,128]{2,1,0:T(8,128)}, f32[1,1152,128]{2,1,0:T(8,128)}) fusion(f32[1152,128]{1,0:T(8,128)S(1)} %reshape.114, f32[1152,384]{1,0:T(8,128)} %fusion.1), kind=kLoop, calls=%fused_computation.27 | loop fusion | flops 2211840 | bytes 4128768 | tf_op jit(solution)/shard_map/broadcast_in_dim | solution.py:96
  190.4 31.1 %reduce-scatter.3.cloned.1.call-done = bf16[256,768]{1,0:T(8,128)(2,1)} async-done(((bf16[1024,768]{1,0:T(8,128)(2,1)}), bf16[256,768]{1,0:T(8,128)(2,1)}) %reduce-scatter.3.cloned.1.call-update) | async-done | bytes 393232 | tf_op jit(solution)/shard_map/reduce_scatter | solution.py:86
  (36 shorter events, 1.2 us)
Async XLA Ops:
  7.2 1.2 copy-start
  7.2 16.0 %copy-start.1 = (f32[1,1152,128]{2,1,0:T(8,128)S(1)}, f32[1,1152,128]{2,1,0:T(8,128)}, u32[]{:S(2)}) copy-start(f32[1,1152,128]{2,1,0:T(8,128)} %param.9) | copy-start | bytes 1769476
  7.2 67.4 %all-gather.5.cloned.1.call-start = ((), (), s32[]{:S(2)}) async-start(), calls=%async_computation.10 | async-start | bytes 3538944 | tf_op jit(solution)/shard_map/all_gather | solution.py:58
  8.4 24.9 %copy-start.6 = (s32[32]{0:T(128)S(1)}, s32[32]{0:T(128)}, u32[]{:S(2)}) copy-start(s32[32]{0:T(128)} %param.12) | copy-start | bytes 388
  24.0 41.3 %copy-start.3 = (bf16[256,768]{1,0:T(8,128)(2,1)S(1)}, bf16[256,768]{1,0:T(8,128)(2,1)}, u32[]{:S(2)}) copy-start(bf16[256,768]{1,0:T(8,128)(2,1)} %param.8) | copy-start | bytes 1179652
  24.0 23.7 %all-to-all-start.1 = ((bf16[32,36,128]{2,1,0:T(8,128)(2,1)}), bf16[32,36,128]{2,1,0:T(8,128)(2,1)S(1)}, u32[]{:S(2)}, u32[]{:S(2)}) async-start(bf16[32,36,128]{2,1,0:T(8,128)(2,1)} %convert_element_type.38), calls=%async_computation.1 | async-start | bytes 655360 | tf_op jit(solution)/shard_map/all_to_all | solution.py:47
  33.2 85.8 %all-gather.7.cloned.1.call-start = ((), (), s32[]{:S(2)}) async-start(), calls=%async_computation.11 | async-start | bytes 2654208 | tf_op jit(solution)/shard_map/all_gather | solution.py:81
  47.8 18.9 %copy-start.4 = (bf16[1152,128]{1,0:T(8,128)(2,1)}, bf16[1152,128]{1,0:T(8,128)(2,1)S(1)}, u32[]{:S(2)}) copy-start(bf16[1152,128]{1,0:T(8,128)(2,1)S(1)} %all_to_all.26) | copy-start | bytes 884740
  66.7 26.5 %all-to-all-start.4 = ((bf16[4,256,768]{2,1,0:T(8,128)(2,1)}), bf16[4,256,768]{2,1,0:T(8,128)(2,1)}, u32[]{:S(2)}, u32[]{:S(2)}) async-start(bf16[4,256,768]{2,1,0:T(8,128)(2,1)} %stack.2), calls=%async_computation.5 | async-start | bytes 3145728 | tf_op jit(solution)/shard_map/all_to_all | solution.py:65
  71.8 104.3 %reduce-scatter.5.cloned.1.call-start = ((), (), s32[]{:S(2)}) async-start(), calls=%async_computation.9 | async-start | bytes 2654208 | tf_op jit(solution)/shard_map/reduce_scatter | solution.py:68
  99.0 122.5 %reduce-scatter.3.cloned.1.call-start = ((), (), s32[]{:S(2)}) async-start(), calls=%async_computation.8 | async-start | bytes 1966080 | tf_op jit(solution)/shard_map/reduce_scatter | solution.py:86
  125.4 1.2 copy-start.2
  126.8 54.0 %copy-start.5 = (bf16[1152,128]{1,0:T(8,128)(2,1)S(1)}, bf16[1152,128]{1,0:T(8,128)(2,1)}, u32[]{:S(2)}) copy-start(bf16[1152,128]{1,0:T(8,128)(2,1)} %copy-done.4) | copy-start | bytes 884740
  176.1 10.9 %all-to-all-start.5 = ((bf16[8,24,768]{2,1,0:T(8,128)(2,1)}), bf16[8,24,768]{2,1,0:T(8,128)(2,1)S(1)}, u32[]{:S(2)}, u32[]{:S(2)}) async-start(bf16[8,24,768]{2,1,0:T(8,128)(2,1)} %bitcast.44), calls=%async_computation.7 | async-start | bytes 589824 | tf_op jit(solution)/shard_map/all_to_all | solution.py:71
Sparse Core Ops, SparseCore 0:
  23.3 51.1 all-gather.4
  76.3 42.6 all-gather.6
  121.6 54.4 reduce-scatter.4
  179.4 42.1 reduce-scatter.2
